TPU v7x, 32 devices: a whole 2x2x4 slice. The times are simulated.
32 devices in a mesh: groups: 2 (over y), ctx: 16 (over z, x, core).
Axes of the slice: x: 2, y: 2, z: 4, core: 2. Of those that a mesh axis runs over, the one named last changes fastest.
Arguments:
- queries: bfloat16 [512, 5120], P(('groups', 'ctx')), parts along dimension 0, may hold values from -45 to 45
- keys: bfloat16 [49152, 1024], P(('groups', 'ctx')), parts along dimension 0, may hold values from -5 to 5
- values: bfloat16 [49152, 1024], P(('groups', 'ctx')), parts along dimension 0, may hold values from -10 to 10
- block_mask: int32 [16, 2, 192], P('groups', None, 'ctx'), parts along dimension 0, may hold values from 0 to 1, as said below
- out_weight: bfloat16 [5120, 5120], P('ctx'), may hold values from -0.078125 to 0.078125
Outputs:
- projected: bfloat16 [512, 5120], P(('groups', 'ctx')), parts along dimension 0
There are 2 independent parts, one for each index of `groups`. A program takes and returns all parts, laid end to end along the dimension named above; an argument that names none is the same for every part. Nothing has to cross between parts.
Inputs may be any that keep to these rules, and one draw needn't show every extreme that they name: `block_mask`: for every key head and query block at least one key block is 1; the share of 1s differs between spans of 1536 positions.
All inputs are finite; a program needn't handle non-finite values.
Results may differ from a plain program's by a relative error of at most 0.0055.
Values may be sent and summed in bfloat16 or wider, within the bound.
A program may use at most 128 MiB of HBM per device.

v0:
```python
import math
import jax
import jax.numpy as jnp
from jax import lax
from jax.sharding import PartitionSpec as P

HEAD_SIZE = 128
NEG = -1e30


def shards(queries, keys, values, block_mask, out_weight):
    whole = lax.all_gather(queries, "ctx", axis=0, tiled=True)
    qtok, width = whole.shape
    kdev = keys.shape[0]
    heads_kv, query_block_count, key_block_count = block_mask.shape
    head_dim = HEAD_SIZE
    query_group = width // head_dim // heads_kv
    scale = 1.0 / math.sqrt(head_dim)
    query_tensor = whole.reshape(qtok, heads_kv, query_group, head_dim)
    key_tensor = keys.reshape(kdev, heads_kv, head_dim)
    value_tensor = values.reshape(kdev, heads_kv, head_dim)

    def head_scores(head):
        q_h = lax.dynamic_index_in_dim(query_tensor, head, 1, keepdims=False)
        k_h = lax.dynamic_index_in_dim(key_tensor, head, 1, keepdims=False)
        scores = jnp.einsum("qge,ke->gqk", q_h, k_h, preferred_element_type=jnp.float32) * scale
        blocks = lax.dynamic_index_in_dim(block_mask, head, 0, keepdims=False)
        live = jnp.broadcast_to(
            blocks[:, None, :, None] > 0,
            (
                query_block_count,
                qtok // query_block_count,
                key_block_count,
                kdev // key_block_count,
            ),
        )
        return (scores, live.reshape(qtok, kdev))

    def max_step(head, maxima):
        scores, live = head_scores(head)
        local = jnp.max(jnp.where(live[None], scores, NEG), axis=2)
        return lax.dynamic_update_slice(maxima, local.T[:, None, :], (0, head, 0))

    maxima = lax.fori_loop(
        0, heads_kv, max_step, jnp.full((qtok, heads_kv, query_group), NEG, jnp.float32)
    )
    row_max = lax.pmax(maxima, "ctx")

    def sum_step(head, carry):
        numer, denom = carry
        scores, live = head_scores(head)
        top = lax.dynamic_index_in_dim(row_max, head, 1, keepdims=False).T[:, :, None]
        probs = jnp.where(live[None], jnp.exp(scores - top), 0.0).astype(jnp.bfloat16)
        total = jnp.sum(probs.astype(jnp.float32), axis=2)
        v_h = lax.dynamic_index_in_dim(value_tensor, head, 1, keepdims=False)
        weighted = jnp.einsum("gqk,ke->qge", probs, v_h, preferred_element_type=jnp.float32)
        numer = lax.dynamic_update_slice(
            numer, weighted.reshape(qtok, 1, query_group * head_dim), (0, head, 0)
        )
        denom = lax.dynamic_update_slice(denom, total.T[:, None, :], (0, head, 0))
        return (numer, denom)

    start_numer = jnp.zeros((qtok, heads_kv, query_group * head_dim), jnp.float32)
    start_denom = jnp.zeros((qtok, heads_kv, query_group), jnp.float32)
    numer, denom = lax.fori_loop(0, heads_kv, sum_step, (start_numer, start_denom))
    numer = numer.reshape(qtok, width)
    denom = denom.reshape(qtok, heads_kv * query_group)
    num_rows, den_rows = (
        lax.psum_scatter(numer, "ctx", scatter_dimension=0, tiled=True),
        lax.psum_scatter(denom, "ctx", scatter_dimension=0, tiled=True),
    )
    own_rows = num_rows.shape[0]
    attn_rows = (num_rows.reshape(own_rows, -1, head_dim) / den_rows[:, :, None]).reshape(
        own_rows, width
    )
    attn_cols = lax.all_to_all(
        attn_rows.astype(jnp.bfloat16), "ctx", split_axis=1, concat_axis=0, tiled=True
    )
    summed = lax.psum_scatter(
        jnp.dot(attn_cols, out_weight, preferred_element_type=jnp.float32),
        "ctx",
        scatter_dimension=0,
        tiled=True,
    )
    return summed.astype(jnp.bfloat16)


def solution(mesh):
    return jax.shard_map(
        shards,
        mesh=mesh,
        in_specs=(
            P(("groups", "ctx"), None),
            P(("groups", "ctx"), None),
            P(("groups", "ctx"), None),
            P("groups", None, "ctx"),
            P("ctx", None),
        ),
        out_specs=P(("groups", "ctx"), None),
        check_vma=False,
    )
```

profile of v0, /device:TPU:0, one launch (start us, length us, event | category | flops | bytes accessed | tf_op | source)
XLA Modules:
  0.0 496.8 jit_solution(2088119072019379952)
XLA Ops:
  7.3 4.9 copy.38
  12.2 4.7 copy.42
  16.9 4.7 copy.37
  21.6 34.0 %all-gather.2.cloned.1.call-done = bf16[256,5120]{1,0:T(8,128)(2,1)} async-done(((bf16[16,5120]{1,0:T(8,128)(2,1)}), bf16[256,5120]{1,0:T(8,128)(2,1)}) %all-gather.2.cloned.1.call-update) | async-done | bytes 2621456 | tf_op jit(solution)/shard_map/all_gather | solution.py:12
  55.6 4.4 copy.39
  60.0 4.3 copy.43
  64.3 53.1 %while.28 = (s32[]{:T(128)}, f32[256,8,5]{0,2,1:T(8,128)S(1)}, s32[8,2,12]{2,1,0:T(2,128)}, bf16[1536,8,128]{2,0,1:T(8,128)(2,1)}, bf16[256,8,5,128]{3,0,2,1:T(8,128)(2,1)}, /*index=5*/s32[]{:T(128)}) while((s32[]{:T(128)}, f32[256,8,5]{0,2,1:T(8,128)S(1)}, s32[8,2,12]{2,1,0:T(2,128)}, bf16[1536,8,128]{2,0,1:T(8,128)(2,1)}, ...), condition=%wide.region_2.3_spmd, body=%wide.region_0.2_spmd.sunk | while | flops 509213472 | bytes 3102949 | solution.py:44
  66.1 2.2 copy.63
  68.4 2.5 fusion.31
  75.0 2.5 fusion.31
  81.6 2.5 fusion.31
  88.3 2.5 fusion.31
  94.9 2.5 fusion.31
  101.5 2.5 fusion.31
  108.2 2.5 fusion.31
  114.8 2.5 fusion.31
  117.4 59.4 %pmax.7 = f32[256,8,5]{0,2,1:T(8,128)S(1)} all-reduce(f32[256,8,5]{0,2,1:T(8,128)S(1)} %get-tuple-element.239), channel_id=1, replica_groups=mesh['groups'=2,'ctx'=16] {'ctx'}, use_global_device_ids=true, to_apply=%region_3.4 | all-reduce | flops 10240 | bytes 81920 | tf_op jit(solution)/shard_map/pmax | solution.py:47
  176.8 80.6 %while.29 = (s32[]{:T(128)}, f32[256,8,640]{0,2,1:T(8,128)}, f32[256,8,5]{0,2,1:T(8,128)S(1)}, bf16[1536,8,128]{0,2,1:T(8,128)(2,1)}, s32[8,2,12]{2,1,0:T(2,128)...) while((s32[]{:T(128)}, f32[256,8,640]{0,2,1:T(8,128)}, ...), condition=%wide.region_6.7_spmd, body=%wide.region_4.6_spmd.sunk | while | flops 1018428160 | bytes 13341961 | solution.py:65
  180.9 3.4 convert_reduce_fusion.2
  190.9 3.4 convert_reduce_fusion.2
  201.0 3.4 convert_reduce_fusion.2
  211.1 3.4 convert_reduce_fusion.2
  221.2 3.4 convert_reduce_fusion.2
  231.3 3.4 convert_reduce_fusion.2
  241.3 3.4 convert_reduce_fusion.2
  251.4 3.4 convert_reduce_fusion.2
  258.3 6.0 %copy.44 = f32[256,5120]{1,0:T(8,128)} copy(f32[256,5120]{0,1:T(8,128)} %bitcast.123) | data formatting | bytes 10485760 | tf_op jit(solution)/shard_map/reshape | solution.py:66
  264.3 46.3 %reduce-scatter.10.cloned.1.call-done = f32[16,40]{1,0:T(8,128)} async-done(((f32[256,40]{1,0:T(8,128)}), f32[16,40]{1,0:T(8,128)}) %reduce-scatter.10.cloned.1.call-update) | async-done | bytes 2576 | tf_op jit(solution)/shard_map/reduce_scatter | solution.py:70
  310.7 81.4 %reduce-scatter.6.cloned.1.call-done = f32[16,5120]{1,0:T(8,128)} async-done(((f32[256,5120]{1,0:T(8,128)}), f32[16,5120]{1,0:T(8,128)}) %reduce-scatter.6.cloned.1.call-update) | async-done | bytes 327696 | tf_op jit(solution)/shard_map/reduce_scatter | solution.py:69
  395.7 12.4 %all_to_all.19 = bf16[16,16,320]{2,0,1:T(8,128)(2,1)S(1)} all-to-all(bf16[16,16,320]{2,0,1:T(8,128)(2,1)S(1)} %copy.46), channel_id=1, replica_groups=mesh['groups'=2,'ctx'=16] {'ctx'}, dimensions={1} | all-to-all | bytes 327680 | tf_op jit(solution)/shard_map/all_to_all | solution.py:76
  408.2 3.9 fusion.19
  412.1 76.6 %reduce-scatter.8.cloned.1.call-done = f32[16,5120]{1,0:T(8,128)} async-done(((f32[256,5120]{1,0:T(8,128)}), f32[16,5120]{1,0:T(8,128)}) %reduce-scatter.8.cloned.1.call-update) | async-done | bytes 327696 | tf_op jit(solution)/shard_map/reduce_scatter | solution.py:79
  (123 shorter events, 90.4 us)
Async XLA Ops:
  6.5 401.6 %copy-start = (bf16[320,5120]{1,0:T(8,128)(2,1)S(1)}, bf16[320,5120]{1,0:T(8,128)(2,1)}, u32[]{:S(2)}) copy-start(bf16[320,5120]{1,0:T(8,128)(2,1)} %param.13) | copy-start | bytes 9830404
  6.5 49.0 %all-gather.2.cloned.1.call-start = ((), (), s32[]{:S(2)}) async-start(), calls=%async_computation.4 | async-start | bytes 2785280 | tf_op jit(solution)/shard_map/all_gather | solution.py:12
  7.3 303.4 %reduce-scatter.10.cloned.1.call-start = ((), (), s32[]{:S(2)}) async-start(), calls=%async_computation.7 | async-start | bytes 139264 | tf_op jit(solution)/shard_map/reduce_scatter | solution.py:70
  258.2 133.8 %reduce-scatter.6.cloned.1.call-start = ((), (), s32[]{:S(2)}) async-start(), calls=%async_computation.5 | async-start | bytes 5570560 | tf_op jit(solution)/shard_map/reduce_scatter | solution.py:69
  264.3 224.4 %reduce-scatter.8.cloned.1.call-start = ((), (), s32[]{:S(2)}) async-start(), calls=%async_computation.6 | async-start | bytes 5570560 | tf_op jit(solution)/shard_map/reduce_scatter | solution.py:79
Sparse Core Ops, SparseCore 0:
  9.6 45.8 all-gather.1
  258.4 52.2 reduce-scatter.9
  314.5 77.4 reduce-scatter.5
  412.2 76.4 reduce-scatter.7
where the time goes:
time: 499 us; the launch traced here: 497 us
  waiting for transfers between devices  239 us (48%)
  local copies, waits for them, and re-layouts  92.9 us (19%)
  blocking collectives  71.9 us (14%)
  matrix products  64.9 us (13%)
  other arithmetic  14.3 us (3%)
  between operations  13.2 us (3%)
    reduce_scatter x1, waiting for transfers between devices, shards(): lax.psum_scatter(numer, 'ctx', scatter_dimension=0, tiled=True)  81.4 us
    reduce_scatter x1, waiting for transfers between devices, shards(): lax.psum_scatter(jnp.dot(attn_cols, out_weight, preferred_element_type=jn...  76.6 us
    pmax x1, blocking collectives, shards(): row_max = lax.pmax(maxima, 'ctx')  59.4 us
    dot_general x16, matrix products, head_scores(): jnp.einsum('qge,ke->gqk', q_h, k_h, preferred_element_type=jnp.float32)  47.6 us
    reduce_scatter x1, waiting for transfers between devices, shards(): lax.psum_scatter(denom, 'ctx', scatter_dimension=0, tiled=True)  46.3 us
    all_gather x1, waiting for transfers between devices, shards(): whole = lax.all_gather(queries, 'ctx', axis=0, tiled=True)  34 us
    broadcast_in_dim x8, local copies, waits for them, and re-layouts, max_step(): local = jnp.max(jnp.where(live[None], scores, NEG), axis=2)  17.8 us
    broadcast_in_dim x8, local copies, waits for them, and re-layouts, sum_step(): jnp.where(live[None], jnp.exp(scores - top), 0.0).astype(jnp.bfloat16)  17.8 us
  transfers between devices with their start and end apart: 4, of which 4 were waited for; matrix products, arithmetic and copies ran while one was open for 4% of the time, Pallas kernels for 0%

commit v1 on v0

--- a/solution.py
+++ b/solution.py
@@ -8,8 +8,20 @@
 NEG = -1e30
 
 
+def collect(x, axis, dim):
+    ways, here = (lax.axis_size(axis), lax.axis_index(axis))
+    grown, reach = (x, 1)
+    while reach < ways:
+        theirs = lax.ppermute(grown, axis, [(d, d ^ reach) for d in range(ways)])
+        mine_first = jnp.concatenate([grown, theirs], axis=dim)
+        theirs_first = jnp.concatenate([theirs, grown], axis=dim)
+        grown = jnp.where(here & reach == 0, mine_first, theirs_first)
+        reach = 2 * reach
+    return grown
+
+
 def shards(queries, keys, values, block_mask, out_weight):
-    whole = lax.all_gather(queries, "ctx", axis=0, tiled=True)
+    whole = collect(queries, "ctx", 0)
     qtok, width = whole.shape
     kdev = keys.shape[0]
     heads_kv, query_block_count, key_block_count = block_mask.shape

time: 499 us -> 572 us (1.15)
  other arithmetic: 14.3 us -> 43.4 us
  local copies, waits for them, and re-layouts: 92.9 us -> 113 us
  waiting for transfers between devices: 239 us -> 253 us
  starting transfers between devices: 0.12 us -> 7.74 us
    ppermute x0 -> x4, waiting for transfers between devices: none -> 49.1 us  [collect(): theirs = lax.ppermute(grown, axis, [(d, d ^ reach) for d in range(ways)])]
    all_gather x1 -> x0, waiting for transfers between devices: 34 us -> none  [shards(): whole = lax.all_gather(queries, 'ctx', axis=0, tiled=True)]
    select_n x0 -> x7, other arithmetic: none -> 27 us  [collect(): grown = jnp.where(here & reach == 0, mine_first, theirs_first)]
    concatenate x0 -> x7, local copies, waits for them, and re-layouts: none -> 16.1 us  [the longest x6 13.8 us: collect(): mine_first = jnp.concatenate([grown, theirs], axis=dim)]
    ppermute x0 -> x4, starting transfers between devices: none -> 7.66 us  [collect(): theirs = lax.ppermute(grown, axis, [(d, d ^ reach) for d in range(ways)])]
  transfers between devices with their start and end apart: 4 -> 7, of which waited for: 4 -> 7; matrix products, arithmetic and copies ran while one was open for 4% -> 7% of each run, Pallas kernels for 0% -> 0%
where the time goes in v1:
time: 572 us; the launch traced here: 570 us
  waiting for transfers between devices  253 us (44%)
  local copies, waits for them, and re-layouts  113 us (20%)
  blocking collectives  73.7 us (13%)
  matrix products  64.9 us (11%)
  other arithmetic  43.4 us (8%)
  between operations  13.2 us (2%)
  starting transfers between devices  7.74 us (1%)
    reduce_scatter x1, waiting for transfers between devices, shards(): lax.psum_scatter(numer, 'ctx', scatter_dimension=0, tiled=True)  81.3 us
    reduce_scatter x1, waiting for transfers between devices, shards(): lax.psum_scatter(jnp.dot(attn_cols, out_weight, preferred_element_type=jn...  76.5 us
    pmax x1, blocking collectives, shards(): row_max = lax.pmax(maxima, 'ctx')  61.2 us
    ppermute x4, waiting for transfers between devices, collect(): theirs = lax.ppermute(grown, axis, [(d, d ^ reach) for d in range(ways)])  49.1 us
    dot_general x16, matrix products, head_scores(): jnp.einsum('qge,ke->gqk', q_h, k_h, preferred_element_type=jnp.float32)  47.6 us
    reduce_scatter x1, waiting for transfers between devices, shards(): lax.psum_scatter(denom, 'ctx', scatter_dimension=0, tiled=True)  46.5 us
    select_n x7, other arithmetic, collect(): grown = jnp.where(here & reach == 0, mine_first, theirs_first)  27 us
    broadcast_in_dim x8, local copies, waits for them, and re-layouts, max_step(): local = jnp.max(jnp.where(live[None], scores, NEG), axis=2)  17.9 us
  transfers between devices with their start and end apart: 7, of which 7 were waited for; matrix products, arithmetic and copies ran while one was open for 7% of the time, Pallas kernels for 0%

profile of v1, /device:TPU:0, one launch (start us, length us, event | category | flops | bytes accessed | tf_op | source)
XLA Modules:
  0.0 569.6 jit_solution(486515067442725495)
XLA Ops:
  19.4 2.9 collective-permute-start.1
  22.3 8.3 %collective-permute-done.1 = bf16[32,5120]{1,0:T(8,128)(2,1)} collective-permute-done((bf16[32,5120]{1,0:T(8,128)(2,1)}, bf16[32,5120]{1,0:T(8,128)(2,1)}, u32[]{:S(2)}, u32[]{:S(2)}) %collective-permute-start.1) | collective-permute-done | bytes 327712 | tf_op jit(solution)/shard_map/ppermute | solution.py:15
  32.9 5.0 maximum_select_fusion.2
  42.0 14.8 %collective-permute-done.2 = bf16[64,5120]{1,0:T(8,128)(2,1)} collective-permute-done((bf16[64,5120]{1,0:T(8,128)(2,1)}, bf16[64,5120]{1,0:T(8,128)(2,1)}, u32[]{:S(2)}, u32[]{:S(2)}) %collective-permute-start.2) | collective-permute-done | bytes 655392 | tf_op jit(solution)/shard_map/ppermute | solution.py:15
  59.0 5.0 maximum_select_fusion.3
  67.7 4.7 copy.52
  72.4 4.7 copy.65
  77.1 4.7 copy.51
  87.8 2.9 maximum_select_fusion.4
  90.8 2.6 concatenate.65
  93.4 4.6 maximum_select_fusion.1
  98.0 24.7 %collective-permute-done.3 = bf16[128,5120]{0,1:T(8,128)(2,1)} collective-permute-done((bf16[128,5120]{0,1:T(8,128)(2,1)}, bf16[128,5120]{0,1:T(8,128)(2,1)}, u32[]{:S(2)}, u32[]{:S(2)}) %collective-permute-start.3) | collective-permute-done | bytes 1310752 | tf_op jit(solution)/shard_map/ppermute | solution.py:15
  122.8 3.8 copy.61
  126.6 4.9 maximum_select_fusion
  131.5 3.6 copy.66
  135.1 53.2 %while.28 = (s32[]{:T(128)}, f32[256,8,5]{0,2,1:T(8,128)S(1)}, s32[8,2,12]{2,1,0:T(2,128)}, bf16[1536,8,128]{2,0,1:T(8,128)(2,1)}, bf16[256,8,5,128]{3,0,2,1:T(8,128)(2,1)}, /*index=5*/s32[]{:T(128)}) while((s32[]{:T(128)}, f32[256,8,5]{0,2,1:T(8,128)S(1)}, s32[8,2,12]{2,1,0:T(2,128)}, bf16[1536,8,128]{2,0,1:T(8,128)(2,1)}, ...), condition=%wide.region_2.3_spmd, body=%wide.region_0.2_spmd.sunk | while | flops 509213472 | bytes 3102949 | solution.py:56
  188.3 61.2 %pmax.7 = f32[256,8,5]{0,2,1:T(8,128)S(1)} all-reduce(f32[256,8,5]{0,2,1:T(8,128)S(1)} %get-tuple-element.239), channel_id=1, replica_groups=mesh['groups'=2,'ctx'=16] {'ctx'}, use_global_device_ids=true, to_apply=%region_3.4 | all-reduce | flops 10240 | bytes 81920 | tf_op jit(solution)/shard_map/pmax | solution.py:59
  249.6 80.7 %while.29 = (s32[]{:T(128)}, f32[256,8,640]{0,2,1:T(8,128)}, f32[256,8,5]{0,2,1:T(8,128)S(1)}, bf16[1536,8,128]{0,2,1:T(8,128)(2,1)}, s32[8,2,12]{2,1,0:T(2,128)...) while((s32[]{:T(128)}, f32[256,8,640]{0,2,1:T(8,128)}, ...), condition=%wide.region_6.7_spmd, body=%wide.region_4.6_spmd.sunk | while | flops 1018428160 | bytes 13341961 | solution.py:77
  253.6 3.4 convert_reduce_fusion.2
  263.7 3.4 convert_reduce_fusion.2
  273.8 3.4 convert_reduce_fusion.2
  283.9 3.4 convert_reduce_fusion.2
  294.0 3.4 convert_reduce_fusion.2
  304.1 3.4 convert_reduce_fusion.2
  314.2 3.4 convert_reduce_fusion.2
  324.3 3.4 convert_reduce_fusion.2
  331.1 5.9 %copy.67 = f32[256,5120]{1,0:T(8,128)} copy(f32[256,5120]{0,1:T(8,128)} %bitcast.122) | data formatting | bytes 10485760 | tf_op jit(solution)/shard_map/reshape | solution.py:78
  337.1 46.5 %reduce-scatter.10.cloned.1.call-done = f32[16,40]{1,0:T(8,128)} async-done(((f32[256,40]{1,0:T(8,128)}), f32[16,40]{1,0:T(8,128)}) %reduce-scatter.10.cloned.1.call-update) | async-done | bytes 2576 | tf_op jit(solution)/shard_map/reduce_scatter | solution.py:82
  383.6 81.3 %reduce-scatter.6.cloned.1.call-done = f32[16,5120]{1,0:T(8,128)} async-done(((f32[256,5120]{1,0:T(8,128)}), f32[16,5120]{1,0:T(8,128)}) %reduce-scatter.6.cloned.1.call-update) | async-done | bytes 327696 | tf_op jit(solution)/shard_map/reduce_scatter | solution.py:81
  468.6 12.5 %all_to_all.19 = bf16[16,16,320]{2,0,1:T(8,128)(2,1)S(1)} all-to-all(bf16[16,16,320]{2,0,1:T(8,128)(2,1)S(1)} %copy.69), channel_id=1, replica_groups=mesh['groups'=2,'ctx'=16] {'ctx'}, dimensions={1} | all-to-all | bytes 327680 | tf_op jit(solution)/shard_map/all_to_all | solution.py:88
  481.1 3.9 fusion.19
  484.9 76.5 %reduce-scatter.8.cloned.1.call-done = f32[16,5120]{1,0:T(8,128)} async-done(((f32[256,5120]{1,0:T(8,128)}), f32[16,5120]{1,0:T(8,128)}) %reduce-scatter.8.cloned.1.call-update) | async-done | bytes 327696 | tf_op jit(solution)/shard_map/reduce_scatter | solution.py:91
  (152 shorter events, 143.7 us)
Async XLA Ops:
  6.5 474.5 %copy-start = (bf16[320,5120]{1,0:T(8,128)(2,1)S(1)}, bf16[320,5120]{1,0:T(8,128)(2,1)}, u32[]{:S(2)}) copy-start(bf16[320,5120]{1,0:T(8,128)(2,1)} %param.13) | copy-start | bytes 9830404
  6.5 377.0 %reduce-scatter.10.cloned.1.call-start = ((), (), s32[]{:S(2)}) async-start(), calls=%async_computation.6 | async-start | bytes 139264 | tf_op jit(solution)/shard_map/reduce_scatter | solution.py:82
  6.5 1.7 collective-permute-start
  8.2 9.0 %copy-start.1 = (bf16[16,5120]{1,0:T(8,128)(2,1)}, bf16[16,5120]{1,0:T(8,128)(2,1)S(1)}, u32[]{:S(2)}) copy-start(bf16[16,5120]{1,0:T(8,128)(2,1)S(1)} %collective-permute-done) | copy-start | bytes 491524
  19.4 11.2 %collective-permute-start.1 = (bf16[32,5120]{1,0:T(8,128)(2,1)}, bf16[32,5120]{1,0:T(8,128)(2,1)}, u32[]{:S(2)}, u32[]{:S(2)}) collective-permute-start(bf16[32,5120]{1,0:T(8,128)(2,1)} %copy.55), channel_id=1, source_target_pairs={{0,2},{1,3},{2,0},{3,1},{4,6},{5,7},{6,4},{7,5},{8,10},{9,11},{10,... | collective-permute-start | bytes 983048 | tf_op jit(solution)/shard_map/ppermute | solution.py:15
  40.1 16.6 %collective-permute-start.2 = (bf16[64,5120]{1,0:T(8,128)(2,1)}, bf16[64,5120]{1,0:T(8,128)(2,1)}, u32[]{:S(2)}, u32[]{:S(2)}) collective-permute-start(bf16[64,5120]{1,0:T(8,128)(2,1)} %copy.58), channel_id=1, source_target_pairs={{0,4},{1,5},{2,6},{3,7},{4,0},{5,1},{6,2},{7,3},{8,12},{9,13},{10,... | collective-permute-start | bytes 1966088 | tf_op jit(solution)/shard_map/ppermute | solution.py:15
  64.0 58.7 %collective-permute-start.3 = (bf16[128,5120]{0,1:T(8,128)(2,1)}, bf16[128,5120]{0,1:T(8,128)(2,1)}, u32[]{:S(2)}, u32[]{:S(2)}) collective-permute-start(bf16[128,5120]{0,1:T(8,128)(2,1)} %maximum_select_fusion.3), channel_id=1, source_target_pairs={{0,8},{1,9},{2,10},{3,11},{4,12},{5,13},{6,14},{7,15},{8,0},{9,1},... | collective-permute-start | bytes 3932168 | tf_op jit(solution)/shard_map/ppermute | solution.py:15
  131.5 3.6 copy-start.2
  135.1 114.5 %copy-start.3 = (f32[256,8,5]{0,2,1:T(8,128)S(1)}, f32[256,8,5]{0,2,1:T(8,128)}, u32[]{:S(2)}) copy-start(f32[256,8,5]{0,2,1:T(8,128)} %custom-call.2) | copy-start | bytes 122884
  331.1 133.8 %reduce-scatter.6.cloned.1.call-start = ((), (), s32[]{:S(2)}) async-start(), calls=%async_computation.4 | async-start | bytes 5570560 | tf_op jit(solution)/shard_map/reduce_scatter | solution.py:81
  337.1 224.3 %reduce-scatter.8.cloned.1.call-start = ((), (), s32[]{:S(2)}) async-start(), calls=%async_computation.5 | async-start | bytes 5570560 | tf_op jit(solution)/shard_map/reduce_scatter | solution.py:91
Sparse Core Ops, SparseCore 0:
  331.2 52.3 reduce-scatter.9
  387.4 77.3 reduce-scatter.5
  485.1 76.3 reduce-scatter.7
